TPU v7x, 32 devices: a whole 2x2x4 slice. The times are simulated.
32 devices in a mesh: dp: 8 (over z, core), expert: 4 (over y, x).
Axes of the slice: x: 2, y: 2, z: 4, core: 2. Of those that a mesh axis runs over, the one named last changes fastest.
Arguments:
- tokens: bfloat16 [24576, 2048], P(('dp', 'expert')), may hold values from -6 to 6
- target: bfloat16 [24576, 2048], P(('dp', 'expert')), may hold values from -4 to 4
- route_index: int32 [8, 4, 4, 16], P('dp', None, 'expert'), may hold values from 0 to 767, as said below
- route_count: int32 [8, 4, 4], P('dp', None, 'expert'), may hold values from 1 to 16, as said below
- route_gate: float32 [8, 4, 4, 16], P('dp', None, 'expert'), may hold values from 0.1 to 1
- gate_weight: bfloat16 [2048, 4, 768], P('dp', 'expert'), may hold values from -0.125 to 0.125
- up_weight: bfloat16 [2048, 4, 768], P('dp', 'expert'), may hold values from -0.125 to 0.125
- down_weight: bfloat16 [2048, 4, 768], P('dp', 'expert'), may hold values from -0.21875 to 0.21875
Outputs:
- token_grad: bfloat16 [24576, 2048], P(('dp', 'expert'))
- gate_gradient: float32 [2048, 4, 768], P('dp', 'expert')
- up_gradient: float32 [2048, 4, 768], P('dp', 'expert')
- down_gradient: float32 [2048, 4, 768], P('dp', 'expert')
Inputs may be any that keep to these rules, and one draw needn't show every extreme that they name: `route_index`: within each list of 16 slots the indices are distinct; each names a token of the source device. `route_count`: in every group one expert has all 16 slots live from every source device; slots at or beyond the count are unused.
All inputs are finite; a program needn't handle non-finite values.
Results may differ from a plain program's by a relative error of at most 0.0059.
Values may be sent and summed in bfloat16 or wider, within the bound.
A program may use at most 128 MiB of HBM per device.

v0:
```python
import jax
import jax.numpy as jnp
from jax import lax
from jax.sharding import PartitionSpec as P


def to_owners(block):
    return lax.all_to_all(block, "expert", split_axis=0, concat_axis=1, tiled=True)


def to_sources(block):
    return lax.all_to_all(block, "expert", split_axis=1, concat_axis=0, tiled=True)


def on_device(
    tokens, target, route_index, route_count, route_gate, gate_weight, up_weight, down_weight
):
    groups = lax.axis_size("dp")
    sources = lax.axis_size("expert")
    local_index = route_index[0, :, 0, :]
    live_count = route_count[0, :, 0]
    per_source = local_index.shape[1]
    model_width = tokens.shape[1]
    usable = jnp.arange(per_source, dtype=jnp.int32)[None, :] < live_count[:, None]
    slot_weight = jnp.where(usable, route_gate[0, :, 0, :], 0.0)
    outgoing = tokens[local_index] * usable[:, :, None].astype(tokens.dtype)
    expert_rows = to_owners(outgoing)
    full_gate, full_up, full_down = (
        lax.all_gather(gate_weight, "dp", axis=0, tiled=True),
        lax.all_gather(up_weight, "dp", axis=0, tiled=True),
        lax.all_gather(down_weight, "dp", axis=0, tiled=True),
    )
    gate_pre = jnp.einsum(
        "erd,def->erf", expert_rows, full_gate, preferred_element_type=jnp.float32
    )
    up_pre = jnp.einsum("erd,def->erf", expert_rows, full_up, preferred_element_type=jnp.float32)
    sigma = jax.nn.sigmoid(gate_pre)
    active = gate_pre * sigma
    hidden = (active * up_pre).astype(jnp.bfloat16)
    expert_out = jnp.einsum(
        "erf,def->erd", hidden, full_down, preferred_element_type=jnp.float32
    ).astype(jnp.bfloat16)
    returned = to_sources(expert_out)
    flat_index = local_index.reshape(-1)
    combined = (
        jnp.zeros((tokens.shape[0], model_width), jnp.float32)
        .at[flat_index]
        .add((slot_weight[:, :, None] * returned.astype(jnp.float32)).reshape(-1, model_width))
    )
    out_grad = combined - target.astype(jnp.float32)
    slot_grad = (slot_weight[:, :, None] * out_grad[local_index]).astype(jnp.bfloat16)
    owner_grad = to_owners(slot_grad)
    hidden_grad = jnp.einsum(
        "erd,def->erf", owner_grad, full_down, preferred_element_type=jnp.float32
    )
    gate_grad = (hidden_grad * up_pre * sigma * (1.0 + gate_pre * (1.0 - sigma))).astype(
        jnp.bfloat16
    )
    up_grad = (hidden_grad * active).astype(jnp.bfloat16)
    row_grad = (
        jnp.einsum("erf,def->erd", gate_grad, full_gate, preferred_element_type=jnp.float32)
        + jnp.einsum("erf,def->erd", up_grad, full_up, preferred_element_type=jnp.float32)
    ).astype(jnp.bfloat16)
    came_back = to_sources(row_grad)
    token_grad = (
        jnp.zeros((tokens.shape[0], model_width), jnp.float32)
        .at[flat_index]
        .add(came_back.astype(jnp.float32).reshape(-1, model_width))
        .astype(jnp.bfloat16)
    )
    factor = (groups * sources * per_source) ** (-0.5)
    rows_every, grad_every = (
        lax.all_to_all(expert_rows, "dp", split_axis=2, concat_axis=1, tiled=True),
        lax.all_to_all(owner_grad, "dp", split_axis=2, concat_axis=1, tiled=True),
    )
    hidden_piece = lax.all_gather(hidden, "dp", axis=1, tiled=True)
    gate_piece = lax.all_gather(gate_grad, "dp", axis=1, tiled=True)
    up_piece = lax.all_gather(up_grad, "dp", axis=1, tiled=True)
    gate_sum = jnp.einsum(
        "erd,erf->def", rows_every, gate_piece, preferred_element_type=jnp.float32
    )
    up_sum = jnp.einsum("erd,erf->def", rows_every, up_piece, preferred_element_type=jnp.float32)
    down_sum = jnp.einsum(
        "erd,erf->def", grad_every, hidden_piece, preferred_element_type=jnp.float32
    )
    gate_gradient = gate_sum * factor
    up_gradient = up_sum * factor
    down_gradient = down_sum * factor
    return (token_grad, gate_gradient, up_gradient, down_gradient)


def solution(mesh):
    return jax.shard_map(
        on_device,
        mesh=mesh,
        in_specs=(
            P(("dp", "expert"), None),
            P(("dp", "expert"), None),
            P("dp", None, "expert", None),
            P("dp", None, "expert"),
            P("dp", None, "expert", None),
            P("dp", "expert", None),
            P("dp", "expert", None),
            P("dp", "expert", None),
        ),
        out_specs=(
            P(("dp", "expert"), None),
            P("dp", "expert", None),
            P("dp", "expert", None),
            P("dp", "expert", None),
        ),
        check_vma=False,
    )
```

profile of v0, /device:TPU:0, one launch (start us, length us, event | category | flops | bytes accessed | tf_op | source)
XLA Modules:
  0.0 305.2 jit_solution(9919206521907058066)
XLA Ops:
  11.8 5.2 %all-to-all-start = ((bf16[4,16,2048]{2,1,0:T(8,128)(2,1)}), bf16[4,16,2048]{2,1,0:T(8,128)(2,1)S(1)}, u32[]{:S(2)}, u32[]{:S(2)}) async-start(bf16[4,16,2048]{2,1,0:T(8,128)(2,1)} %broadcast_multiply_fusion), calls=%async_computation | async-start | bytes 524288 | tf_op jit(solution)/shard_map/all_to_all | solution.py:8
  18.3 4.1 %all-to-all-done = bf16[4,16,2048]{2,1,0:T(8,128)(2,1)S(1)} async-done(((bf16[4,16,2048]{2,1,0:T(8,128)(2,1)}), bf16[4,16,2048]{2,1,0:T(8,128)(2,1)S(1)}, u32[]{:S(2)}, u32[]{:S(2)}) %all-to-all-start) | async-done | bytes 262176 | tf_op jit(solution)/shard_map/all_to_all | solution.py:8
  24.9 13.3 %reduce.10 = bf16[2048,64]{1,0:T(8,128)(2,1)} reduce(bf16[2048,1,64]{2,1,0:T(2,128)(2,1)} %bitcast.114, bf16[]{:T(256)} %broadcast.134), dimensions={1}, to_apply=%bitcast.86.reduce_sub_computation | reduce | bytes 524290
  40.3 4.9 %all-to-all-start.4 = ((bf16[8,2,8192]{2,1,0:T(2,128)(2,1)}), bf16[8,2,8192]{2,1,0:T(2,128)(2,1)}, u32[]{:S(2)}, u32[]{:S(2)}) async-start(bf16[8,2,8192]{2,1,0:T(2,128)(2,1)} %reshape.301), calls=%async_computation.4 | async-start | bytes 524288 | tf_op jit(solution)/shard_map/all_to_all | solution.py:73
  46.6 8.4 %all-to-all-done.4 = bf16[8,2,8192]{2,1,0:T(2,128)(2,1)} async-done(((bf16[8,2,8192]{2,1,0:T(2,128)(2,1)}), bf16[8,2,8192]{2,1,0:T(2,128)(2,1)}, u32[]{:S(2)}, u32[]{:S(2)}) %all-to-all-start.4) | async-done | bytes 262176 | tf_op jit(solution)/shard_map/all_to_all | solution.py:73
  58.4 3.4 %copy.41 = bf16[1,64,2048]{2,1,0:T(8,128)(2,1)} copy(bf16[1,64,2048]{1,0,2:T(2,128)(2,1)} %bitcast.112) | data formatting | bytes 524288 | tf_op jit(solution)/shard_map/all_to_all | solution.py:73
  66.8 24.2 %all-gather.9.cloned.1.call-done = bf16[2048,1,768]{2,0,1:T(8,128)(2,1)} async-done(((bf16[256,1,768]{2,0,1:T(8,128)(2,1)}), bf16[2048,1,768]{2,0,1:T(8,128)(2,1)}) %all-gather.9.cloned.1.call-update) | async-done | bytes 3145744 | tf_op jit(solution)/shard_map/all_gather | solution.py:30
  94.1 35.6 %all-gather.11.cloned.1.call-done = bf16[2048,1,768]{2,0,1:T(8,128)(2,1)} async-done(((bf16[256,1,768]{2,0,1:T(8,128)(2,1)}), bf16[2048,1,768]{2,0,1:T(8,128)(2,1)}) %all-gather.11.cloned.1.call-update) | async-done | bytes 3145744 | tf_op jit(solution)/shard_map/all_gather | solution.py:31
  133.9 3.8 %reduce.8 = bf16[64,2048]{1,0:T(8,128)(2,1)} reduce(bf16[64,1,2048]{2,1,0:T(2,128)(2,1)} %bitcast.123, bf16[]{:T(256)} %broadcast.134), dimensions={1}, to_apply=%bitcast.109.reduce_sub_computation | reduce | bytes 524290
  139.5 4.2 %all-to-all-start.1 = ((bf16[4,2,16384]{2,1,0:T(2,128)(2,1)}), bf16[4,2,16384]{2,1,0:T(2,128)(2,1)}, u32[]{:S(2)}, u32[]{:S(2)}) async-start(bf16[4,2,16384]{2,1,0:T(2,128)(2,1)} %reshape.297), calls=%async_computation.1 | async-start | bytes 524288 | tf_op jit(solution)/shard_map/all_to_all | solution.py:12
  143.8 5.8 %all-to-all-done.1 = bf16[4,2,16384]{2,1,0:T(2,128)(2,1)} async-done(((bf16[4,2,16384]{2,1,0:T(2,128)(2,1)}), bf16[4,2,16384]{2,1,0:T(2,128)(2,1)}, u32[]{:S(2)}, u32[]{:S(2)}) %all-to-all-start.1) | async-done | bytes 262176 | tf_op jit(solution)/shard_map/all_to_all | solution.py:12
  151.5 5.1 %scatter_custom_fusion = f32[768,2048]{1,0:T(8,128)} fusion(s32[64]{0:T(128)S(1)} %fusion.41, f32[]{:T(128)} %constant.5.clone.1, bf16[1,64,2048]{2,0,1:T(2,128)(2,1)} %bitcast.122, f32[64]{0:T(128)S(1)} %broadcast_select_fusion.1), kind=kCustom, calls=%fused_computation.19 | custom fusion | flops 393216 | bytes 6554116 | tf_op jit(solution)/shard_map/scatter-add | solution.py:48
  156.6 7.9 %convert_subtract_fusion = f32[768,2048]{1,0:T(8,128)} fusion(f32[768,2048]{1,0:T(8,128)} %scatter_custom_fusion, bf16[768,2048]{1,0:T(8,128)(2,1)} %param.9), kind=kLoop, calls=%fused_computation.4 | loop fusion | flops 3145728 | bytes 15728640 | tf_op jit(solution)/shard_map/sub | solution.py:50
  164.4 4.6 %gather_fusion.1 = f32[64,2048]{1,0:T(8,128)} fusion(f32[768,2048]{1,0:T(8,128)} %convert_subtract_fusion, s32[1024]{0:T(1024)S(1)} %pad_clamp_fusion), kind=kCustom, calls=%fused_computation.1 | custom fusion | bytes 1048832 | tf_op jit(solution)/shard_map/gather | solution.py:51
  170.8 4.1 %all-to-all-start.2 = ((bf16[4,16,2048]{2,1,0:T(8,128)(2,1)}), bf16[4,16,2048]{2,1,0:T(8,128)(2,1)}, u32[]{:S(2)}, u32[]{:S(2)}) async-start(bf16[4,16,2048]{2,1,0:T(8,128)(2,1)} %multiply_convert_fusion), calls=%async_computation.2 | async-start | bytes 524288 | tf_op jit(solution)/shard_map/all_to_all | solution.py:8
  174.9 16.5 %all-gather.2 = bf16[512,768]{1,0:T(8,128)(2,1)} all-gather(bf16[64,768]{1,0:T(8,128)(2,1)S(1)} %get-tuple-element.28), channel_id=4, replica_groups=mesh['dp'=8,'expert'=4] {'dp'}, dimensions={0}, use_global_device_ids=true | all-gather | bytes 884736 | tf_op jit(solution)/shard_map/all_gather | solution.py:76
  197.7 3.8 %reduce.9 = bf16[64,2048]{1,0:T(8,128)(2,1)} reduce(bf16[64,1,2048]{2,1,0:T(2,128)(2,1)} %bitcast.124, bf16[]{:T(256)} %broadcast.134), dimensions={1}, to_apply=%bitcast.108.reduce_sub_computation | reduce | bytes 524290
  203.4 4.2 %all-to-all-start.3 = ((bf16[4,2,16384]{2,1,0:T(2,128)(2,1)}), bf16[4,2,16384]{2,1,0:T(2,128)(2,1)}, u32[]{:S(2)}, u32[]{:S(2)}) async-start(bf16[4,2,16384]{2,1,0:T(2,128)(2,1)} %reshape.299), calls=%async_computation.3 | async-start | bytes 524288 | tf_op jit(solution)/shard_map/all_to_all | solution.py:12
  207.6 16.5 %all-gather = bf16[512,768]{1,0:T(8,128)(2,1)S(1)} all-gather(bf16[64,768]{1,0:T(8,128)(2,1)} %copy-done.4), channel_id=2, replica_groups=mesh['dp'=8,'expert'=4] {'dp'}, dimensions={0}, use_global_device_ids=true | all-gather | bytes 884736 | tf_op jit(solution)/shard_map/all_gather | solution.py:77
  231.8 13.3 %reduce.11 = bf16[2048,64]{1,0:T(8,128)(2,1)} reduce(bf16[2048,1,64]{2,1,0:T(2,128)(2,1)} %bitcast.115, bf16[]{:T(256)} %broadcast.134), dimensions={1}, to_apply=%bitcast.88.reduce_sub_computation | reduce | bytes 524290
  247.3 4.1 %all-to-all-start.5 = ((bf16[8,2,8192]{2,1,0:T(2,128)(2,1)}), bf16[8,2,8192]{2,1,0:T(2,128)(2,1)}, u32[]{:S(2)}, u32[]{:S(2)}) async-start(bf16[8,2,8192]{2,1,0:T(2,128)(2,1)} %reshape.303), calls=%async_computation.5 | async-start | bytes 524288 | tf_op jit(solution)/shard_map/all_to_all | solution.py:74
  251.3 19.9 %all-gather.1 = bf16[512,768]{1,0:T(8,128)(2,1)S(1)} all-gather(bf16[64,768]{1,0:T(8,128)(2,1)S(1)} %get-tuple-element.25), channel_id=3, replica_groups=mesh['dp'=8,'expert'=4] {'dp'}, dimensions={0}, use_global_device_ids=true | all-gather | bytes 884736 | tf_op jit(solution)/shard_map/all_gather | solution.py:78
  277.5 5.1 %scatter_custom_fusion.1 = f32[768,2048]{1,0:T(8,128)} fusion(s32[64]{0:T(128)S(1)} %fusion.41, f32[]{:T(128)} %constant.5.clone.1, bf16[1,64,2048]{2,0,1:T(2,128)(2,1)} %bitcast.125), kind=kCustom, calls=%fused_computation.17 | custom fusion | flops 262144 | bytes 6553604 | tf_op jit(solution)/shard_map/scatter-add | solution.py:68
  282.5 4.9 %convert_element_type.75 = bf16[768,2048]{1,0:T(8,128)(2,1)} convert(f32[768,2048]{1,0:T(8,128)} %scatter_custom_fusion.1) | non-fusion elementwise | flops 1572864 | bytes 9437184 | tf_op jit(solution)/shard_map/convert_element_type | solution.py:69
  (75 shorter events, 68.6 us)
Async XLA Ops:
  7.2 3.0 copy-start
  7.2 10.4 %copy-start.5 = (s32[1,4,1,16]{3,2,1,0:T(1,128)S(1)}, s32[1,4,1,16]{3,2,1,0:T(1,128)}, u32[]{:S(2)}) copy-start(s32[1,4,1,16]{3,2,1,0:T(1,128)} %param.10) | copy-start | bytes 772
  7.2 3.8 %copy-start.7 = (s32[1,4,1]{1,2,0:T(1,128)S(1)}, s32[1,4,1]{1,2,0:T(1,128)}, u32[]{:S(2)}) copy-start(s32[1,4,1]{1,2,0:T(1,128)} %param.11) | copy-start | bytes 52
  7.2 56.3 %all-gather.7.cloned.1.call-start = ((), (), s32[]{:S(2)}) async-start(), calls=%async_computation.6 | async-start | bytes 3538944 | tf_op jit(solution)/shard_map/all_gather | solution.py:29
  7.9 83.0 %all-gather.9.cloned.1.call-start = ((), (), s32[]{:S(2)}) async-start(), calls=%async_computation.7 | async-start | bytes 3538944 | tf_op jit(solution)/shard_map/all_gather | solution.py:30
  8.7 121.0 %all-gather.11.cloned.1.call-start = ((), (), s32[]{:S(2)}) async-start(), calls=%async_computation.8 | async-start | bytes 3538944 | tf_op jit(solution)/shard_map/all_gather | solution.py:31
  10.9 34.9 %copy-start.6 = (f32[1,4,1,16]{3,2,1,0:T(1,128)S(1)}, f32[1,4,1,16]{3,2,1,0:T(1,128)}, u32[]{:S(2)}) copy-start(f32[1,4,1,16]{3,2,1,0:T(1,128)} %param.12) | copy-start | bytes 772
  11.8 10.6 %all-to-all-start = ((bf16[4,16,2048]{2,1,0:T(8,128)(2,1)}), bf16[4,16,2048]{2,1,0:T(8,128)(2,1)S(1)}, u32[]{:S(2)}, u32[]{:S(2)}) async-start(bf16[4,16,2048]{2,1,0:T(8,128)(2,1)} %broadcast_multiply_fusion), calls=%async_computation | async-start | bytes 524288 | tf_op jit(solution)/shard_map/all_to_all | solution.py:8
  40.3 14.7 %all-to-all-start.4 = ((bf16[8,2,8192]{2,1,0:T(2,128)(2,1)}), bf16[8,2,8192]{2,1,0:T(2,128)(2,1)}, u32[]{:S(2)}, u32[]{:S(2)}) async-start(bf16[8,2,8192]{2,1,0:T(2,128)(2,1)} %reshape.301), calls=%async_computation.4 | async-start | bytes 524288 | tf_op jit(solution)/shard_map/all_to_all | solution.py:73
  94.1 49.6 %copy-start.3 = (bf16[8,8,8,256]{3,2,1,0:T(8,128)(2,1)S(1)}, bf16[8,8,8,256]{3,2,1,0:T(8,128)(2,1)}, u32[]{:S(2)}) copy-start(bf16[8,8,8,256]{3,2,1,0:T(8,128)(2,1)} %copy.49) | copy-start | bytes 786436
  139.5 10.2 %all-to-all-start.1 = ((bf16[4,2,16384]{2,1,0:T(2,128)(2,1)}), bf16[4,2,16384]{2,1,0:T(2,128)(2,1)}, u32[]{:S(2)}, u32[]{:S(2)}) async-start(bf16[4,2,16384]{2,1,0:T(2,128)(2,1)} %reshape.297), calls=%async_computation.1 | async-start | bytes 524288 | tf_op jit(solution)/shard_map/all_to_all | solution.py:12
  170.8 20.5 %all-to-all-start.2 = ((bf16[4,16,2048]{2,1,0:T(8,128)(2,1)}), bf16[4,16,2048]{2,1,0:T(8,128)(2,1)}, u32[]{:S(2)}, u32[]{:S(2)}) async-start(bf16[4,16,2048]{2,1,0:T(8,128)(2,1)} %multiply_convert_fusion), calls=%async_computation.2 | async-start | bytes 524288 | tf_op jit(solution)/shard_map/all_to_all | solution.py:8
  191.4 3.0 copy-start.2
  191.4 4.1 %copy-start.1 = (bf16[2048,1,768]{2,0,1:T(8,128)(2,1)S(1)}, bf16[2048,1,768]{2,0,1:T(8,128)(2,1)}, u32[]{:S(2)}) copy-start(bf16[2048,1,768]{2,0,1:T(8,128)(2,1)} %all-gather.7.cloned.1.call-done) | copy-start | bytes 9437188
  194.2 2.3 copy-start.4
  203.4 43.9 %all-to-all-start.3 = ((bf16[4,2,16384]{2,1,0:T(2,128)(2,1)}), bf16[4,2,16384]{2,1,0:T(2,128)(2,1)}, u32[]{:S(2)}, u32[]{:S(2)}) async-start(bf16[4,2,16384]{2,1,0:T(2,128)(2,1)} %reshape.299), calls=%async_computation.3 | async-start | bytes 524288 | tf_op jit(solution)/shard_map/all_to_all | solution.py:12
  247.3 40.2 %all-to-all-start.5 = ((bf16[8,2,8192]{2,1,0:T(2,128)(2,1)}), bf16[8,2,8192]{2,1,0:T(2,128)(2,1)}, u32[]{:S(2)}, u32[]{:S(2)}) async-start(bf16[8,2,8192]{2,1,0:T(2,128)(2,1)} %reshape.303), calls=%async_computation.5 | async-start | bytes 524288 | tf_op jit(solution)/shard_map/all_to_all | solution.py:74
Sparse Core Ops, SparseCore 0:
  9.6 40.9 all-gather.6
  52.3 38.6 all-gather.8
  92.6 37.1 all-gather.10
where the time goes:
time: 307 us; the launch traced here: 305 us
  waiting for transfers between devices  80.1 us (26%)
  other arithmetic  62 us (20%)
  blocking collectives  52.9 us (17%)
  local copies, waits for them, and re-layouts  50.3 us (16%)
  starting transfers between devices  26.7 us (9%)
  matrix products  19.3 us (6%)
  between operations  13.9 us (5%)
    all_gather x1, waiting for transfers between devices, on_device(): lax.all_gather(down_weight, 'dp', axis=0, tiled=True)  35.6 us
    unnamed x6, other arithmetic  35.6 us
    unnamed x32, local copies, waits for them, and re-layouts  31.1 us
    all_gather x1, waiting for transfers between devices, on_device(): lax.all_gather(up_weight, 'dp', axis=0, tiled=True)  24.2 us
    all_gather x1, blocking collectives, on_device(): up_piece = lax.all_gather(up_grad, 'dp', axis=1, tiled=True)  19.9 us
    all_gather x1, blocking collectives, on_device(): gate_piece = lax.all_gather(gate_grad, 'dp', axis=1, tiled=True)  16.5 us
    all_gather x1, blocking collectives, on_device(): hidden_piece = lax.all_gather(hidden, 'dp', axis=1, tiled=True)  16.5 us
    all_to_all x2, starting transfers between devices, to_owners(): lax.all_to_all(block, 'expert', split_axis=0, concat_axis=1, tiled=True)  9.24 us
  transfers between devices with their start and end apart: 9, of which 5 were waited for; matrix products, arithmetic and copies ran while one was open for 25% of the time, Pallas kernels for 0%

commit v1 on v0

--- a/solution.py
+++ b/solution.py
@@ -2,6 +2,22 @@
 import jax.numpy as jnp
 from jax import lax
 from jax.sharding import PartitionSpec as P
+
+
+def product_in_turn(value, axis, dim, contribution):
+    count, index, rows = (lax.axis_size(axis), lax.axis_index(axis), value.shape[dim])
+    right = [(i, (i + 1) % count) for i in range(count)]
+    left = [(i, (i - 1) % count) for i in range(count)]
+    half = count // 2
+    from_left = from_right = value
+    subtotal = contribution(value, index * rows)
+    for step in range(1, half + 1):
+        from_left = lax.ppermute(from_left, axis, right)
+        if step < count - half:
+            from_right = lax.ppermute(from_right, axis, left)
+            subtotal = subtotal + contribution(from_right, (index + step) % count * rows)
+        subtotal = subtotal + contribution(from_left, (index - step) % count * rows)
+    return subtotal
 
 
 def to_owners(block):
@@ -75,11 +91,20 @@
     )
     hidden_piece = lax.all_gather(hidden, "dp", axis=1, tiled=True)
     gate_piece = lax.all_gather(gate_grad, "dp", axis=1, tiled=True)
-    up_piece = lax.all_gather(up_grad, "dp", axis=1, tiled=True)
     gate_sum = jnp.einsum(
         "erd,erf->def", rows_every, gate_piece, preferred_element_type=jnp.float32
     )
-    up_sum = jnp.einsum("erd,erf->def", rows_every, up_piece, preferred_element_type=jnp.float32)
+    up_sum = product_in_turn(
+        up_grad,
+        "dp",
+        1,
+        lambda shard, offset: jnp.einsum(
+            "erd,erf->def",
+            lax.dynamic_slice_in_dim(rows_every, offset, shard.shape[1], axis=1),
+            shard,
+            preferred_element_type=jnp.float32,
+        ),
+    )
     down_sum = jnp.einsum(
         "erd,erf->def", grad_every, hidden_piece, preferred_element_type=jnp.float32
     )

time: 307 us -> 292 us (0.951)
  waiting for transfers between devices: 80.1 us -> 102 us
  local copies, waits for them, and re-layouts: 50.3 us -> 29.5 us
  blocking collectives: 52.9 us -> 32.8 us
  starting transfers between devices: 26.7 us -> 36.3 us
  other arithmetic: 62 us -> 53.7 us
    all_gather x1 -> x0, blocking collectives: 19.9 us -> none  [on_device(): up_piece = lax.all_gather(up_grad, 'dp', axis=1, tiled=True)]
    unnamed x32 -> x36, local copies, waits for them, and re-layouts: 31.1 us -> 16.8 us
    all_gather x1, waiting for transfers between devices: 24.2 us -> 36 us  [on_device(): lax.all_gather(up_weight, 'dp', axis=0, tiled=True)]
    ppermute x0 -> x7, starting transfers between devices: none -> 10.8 us  [the longest x3 9.62 us: product_in_turn(): from_right = lax.ppermute(from_right, axis, left)]
    unnamed x6, other arithmetic: 35.6 us -> 28.6 us
    ppermute x0 -> x7, waiting for transfers between devices: none -> 6.21 us  [the longest x4 5.32 us: product_in_turn(): from_left = lax.ppermute(from_left, axis, right)]
    dot_general x1 -> x8, matrix products: 1.29 us -> 4.97 us  [on_device(): jnp.einsum('erd,erf->def', lax.dynamic_slice_in_dim(rows_every, offset, s...]
    all_to_all x1, waiting for transfers between devices: 8.38 us -> 12 us  [on_device(): lax.all_to_all(expert_rows, 'dp', split_axis=2, concat_axis=1, tiled=True)]
  transfers between devices with their start and end apart: 9 -> 16, of which waited for: 5 -> 8; matrix products, arithmetic and copies ran while one was open for 25% -> 23% of each run, Pallas kernels for 0% -> 0%
where the time goes in v1:
time: 292 us; the launch traced here: 291 us
  waiting for transfers between devices  102 us (35%)
  other arithmetic  53.7 us (18%)
  starting transfers between devices  36.3 us (12%)
  blocking collectives  32.8 us (11%)
  local copies, waits for them, and re-layouts  29.5 us (10%)
  matrix products  22.3 us (8%)
  between operations  14.2 us (5%)
    all_gather x1, waiting for transfers between devices, on_device(): lax.all_gather(up_weight, 'dp', axis=0, tiled=True)  36 us
    all_gather x1, waiting for transfers between devices, on_device(): lax.all_gather(down_weight, 'dp', axis=0, tiled=True)  35.6 us
    unnamed x6, other arithmetic  28.6 us
    unnamed x36, local copies, waits for them, and re-layouts  16.8 us
    all_gather x1, blocking collectives, on_device(): hidden_piece = lax.all_gather(hidden, 'dp', axis=1, tiled=True)  16.5 us
    all_gather x1, blocking collectives, on_device(): gate_piece = lax.all_gather(gate_grad, 'dp', axis=1, tiled=True)  16.4 us
    all_to_all x1, waiting for transfers between devices, on_device(): lax.all_to_all(expert_rows, 'dp', split_axis=2, concat_axis=1, tiled=True)  12 us
    ppermute x3, starting transfers between devices, product_in_turn(): from_right = lax.ppermute(from_right, axis, left)  9.62 us
  transfers between devices with their start and end apart: 16, of which 8 were waited for; matrix products, arithmetic and copies ran while one was open for 23% of the time, Pallas kernels for 0%

profile of v1, /device:TPU:0, one launch (start us, length us, event | category | flops | bytes accessed | tf_op | source)
XLA Modules:
  0.0 290.5 jit_solution(14955747990581886196)
XLA Ops:
  11.8 5.2 %all-to-all-start = ((bf16[4,16,2048]{2,1,0:T(8,128)(2,1)}), bf16[4,16,2048]{2,1,0:T(8,128)(2,1)S(1)}, u32[]{:S(2)}, u32[]{:S(2)}) async-start(bf16[4,16,2048]{2,1,0:T(8,128)(2,1)} %broadcast_multiply_fusion), calls=%async_computation | async-start | bytes 524288 | tf_op jit(solution)/shard_map/all_to_all | solution.py:24
  18.3 4.1 %all-to-all-done = bf16[4,16,2048]{2,1,0:T(8,128)(2,1)S(1)} async-done(((bf16[4,16,2048]{2,1,0:T(8,128)(2,1)}), bf16[4,16,2048]{2,1,0:T(8,128)(2,1)S(1)}, u32[]{:S(2)}, u32[]{:S(2)}) %all-to-all-start) | async-done | bytes 262176 | tf_op jit(solution)/shard_map/all_to_all | solution.py:24
  23.7 11.5 %reduce.10 = bf16[2048,64]{1,0:T(8,128)(2,1)S(1)} reduce(bf16[2048,1,64]{2,1,0:T(2,128)(2,1)S(1)} %bitcast.160, bf16[]{:T(256)} %broadcast.145), dimensions={1}, to_apply=%bitcast.133.reduce_sub_computation | reduce | bytes 524290
  36.3 4.9 %all-to-all-start.4 = ((bf16[8,2,8192]{2,1,0:T(2,128)(2,1)}), bf16[8,2,8192]{2,1,0:T(2,128)(2,1)S(1)}, u32[]{:S(2)}, u32[]{:S(2)}) async-start(bf16[8,2,8192]{2,1,0:T(2,128)(2,1)} %reshape.369), calls=%async_computation.4 | async-start | bytes 524288 | tf_op jit(solution)/shard_map/all_to_all | solution.py:89
  42.7 12.0 %all-to-all-done.4 = bf16[8,2,8192]{2,1,0:T(2,128)(2,1)S(1)} async-done(((bf16[8,2,8192]{2,1,0:T(2,128)(2,1)}), bf16[8,2,8192]{2,1,0:T(2,128)(2,1)S(1)}, u32[]{:S(2)}, u32[]{:S(2)}) %all-to-all-start.4) | async-done | bytes 262176 | tf_op jit(solution)/shard_map/all_to_all | solution.py:89
  58.6 36.0 %all-gather.8.cloned.1.call-done = bf16[2048,1,768]{2,0,1:T(8,128)(2,1)} async-done(((bf16[256,1,768]{2,0,1:T(8,128)(2,1)}), bf16[2048,1,768]{2,0,1:T(8,128)(2,1)}) %all-gather.8.cloned.1.call-update) | async-done | bytes 3145744 | tf_op jit(solution)/shard_map/all_gather | solution.py:46
  94.6 3.2 %multiply_convert_fusion.3 = (bf16[64,768]{1,0:T(8,128)(2,1)S(1)}, f32[64,768]{1,0:T(8,128)}) fusion(f32[64,768]{1,0:T(8,128)S(1)} %fusion.10, bf16[64,2048]{1,0:T(8,128)(2,1)S(1)} %bitcast.164, bf16[2048,1,768]{2,0,1:T(8,128)(2,1)} %all-gather.8.cloned.1.call-done), kind=kOutput, calls=%fused_computation.51 | convolution fusion | flops 201621504 | bytes 3899392 | tf_op jit(solution)/shard_map/erd,def->erf/dot_general | solution.py:52
  97.8 35.6 %all-gather.10.cloned.1.call-done = bf16[2048,1,768]{2,0,1:T(8,128)(2,1)} async-done(((bf16[256,1,768]{2,0,1:T(8,128)(2,1)}), bf16[2048,1,768]{2,0,1:T(8,128)(2,1)}) %all-gather.10.cloned.1.call-update) | async-done | bytes 3145744 | tf_op jit(solution)/shard_map/all_gather | solution.py:47
  139.8 3.6 %all-to-all-start.1 = ((bf16[4,2,16384]{2,1,0:T(2,128)(2,1)}), bf16[4,2,16384]{2,1,0:T(2,128)(2,1)S(1)}, u32[]{:S(2)}, u32[]{:S(2)}) async-start(bf16[4,2,16384]{2,1,0:T(2,128)(2,1)} %reshape.365), calls=%async_computation.1 | async-start | bytes 524288 | tf_op jit(solution)/shard_map/all_to_all | solution.py:28
  143.5 5.7 %all-to-all-done.1 = bf16[4,2,16384]{2,1,0:T(2,128)(2,1)S(1)} async-done(((bf16[4,2,16384]{2,1,0:T(2,128)(2,1)}), bf16[4,2,16384]{2,1,0:T(2,128)(2,1)S(1)}, u32[]{:S(2)}, u32[]{:S(2)}) %all-to-all-start.1) | async-done | bytes 262176 | tf_op jit(solution)/shard_map/all_to_all | solution.py:28
  150.1 5.3 %scatter_custom_fusion = f32[768,2048]{1,0:T(8,128)} fusion(s32[64]{0:T(128)S(1)} %fusion.78, f32[]{:T(128)} %constant.57.clone.1, bf16[1,64,2048]{2,0,1:T(2,128)(2,1)} %bitcast.175, f32[64]{0:T(128)S(1)} %broadcast_select_fusion.1), kind=kCustom, calls=%fused_computation.19 | custom fusion | flops 393216 | bytes 6554116 | tf_op jit(solution)/shard_map/scatter-add | solution.py:64
  155.4 6.9 %convert_subtract_fusion = f32[768,2048]{1,0:T(8,128)} fusion(f32[768,2048]{1,0:T(8,128)} %scatter_custom_fusion, bf16[768,2048]{1,0:T(8,128)(2,1)S(1)} %copy-done.5), kind=kLoop, calls=%fused_computation.4 | loop fusion | flops 3145728 | bytes 15728640 | tf_op jit(solution)/shard_map/sub | solution.py:66
  162.3 4.7 %gather_fusion.1 = f32[64,2048]{1,0:T(8,128)} fusion(f32[768,2048]{1,0:T(8,128)} %convert_subtract_fusion, s32[1024]{0:T(1024)S(1)} %pad_clamp_fusion), kind=kCustom, calls=%fused_computation.1 | custom fusion | bytes 1048832 | tf_op jit(solution)/shard_map/gather | solution.py:67
  168.9 4.1 %all-to-all-start.2 = ((bf16[4,16,2048]{2,1,0:T(8,128)(2,1)}), bf16[4,16,2048]{2,1,0:T(8,128)(2,1)}, u32[]{:S(2)}, u32[]{:S(2)}) async-start(bf16[4,16,2048]{2,1,0:T(8,128)(2,1)} %multiply_convert_fusion), calls=%async_computation.2 | async-start | bytes 524288 | tf_op jit(solution)/shard_map/all_to_all | solution.py:24
  172.9 16.5 %all-gather.1 = bf16[512,768]{1,0:T(8,128)(2,1)} all-gather(bf16[64,768]{1,0:T(8,128)(2,1)S(1)} %get-tuple-element.28), channel_id=3, replica_groups=mesh['dp'=8,'expert'=4] {'dp'}, dimensions={0}, use_global_device_ids=true | all-gather | bytes 884736 | tf_op jit(solution)/shard_map/all_gather | solution.py:92
  191.6 3.2 %collective-permute-start = (bf16[1,64,768]{2,1,0:T(8,128)(2,1)S(1)}, bf16[1,64,768]{2,1,0:T(8,128)(2,1)}, u32[]{:S(2)}, u32[]{:S(2)}) collective-permute-start(bf16[1,64,768]{2,1,0:T(8,128)(2,1)S(1)} %bitcast.186), channel_id=1, source_target_pairs={{0,28},{4,0},{8,4},{12,8},{16,12},{20,16},{24,20},{28,24},{1,29},{... | collective-permute-start | bytes 294920 | tf_op jit(solution)/shard_map/ppermute | solution.py:17
  194.8 16.4 %all-gather = bf16[512,768]{1,0:T(8,128)(2,1)} all-gather(bf16[64,768]{1,0:T(8,128)(2,1)S(1)} %get-tuple-element.24), channel_id=2, replica_groups=mesh['dp'=8,'expert'=4] {'dp'}, dimensions={0}, use_global_device_ids=true | all-gather | bytes 884736 | tf_op jit(solution)/shard_map/all_gather | solution.py:93
  218.6 4.3 %all-to-all-start.3 = ((bf16[4,2,16384]{2,1,0:T(2,128)(2,1)}), bf16[4,2,16384]{2,1,0:T(2,128)(2,1)}, u32[]{:S(2)}, u32[]{:S(2)}) async-start(bf16[4,2,16384]{2,1,0:T(2,128)(2,1)} %reshape.367), calls=%async_computation.3 | async-start | bytes 524288 | tf_op jit(solution)/shard_map/all_to_all | solution.py:28
  227.5 11.5 %reduce.11 = bf16[2048,64]{1,0:T(8,128)(2,1)S(1)} reduce(bf16[2048,1,64]{2,1,0:T(2,128)(2,1)S(1)} %bitcast.161, bf16[]{:T(256)} %broadcast.145), dimensions={1}, to_apply=%bitcast.135.reduce_sub_computation | reduce | bytes 524290
  246.1 3.4 %all-to-all-start.5 = ((bf16[8,2,8192]{2,1,0:T(2,128)(2,1)}), bf16[8,2,8192]{2,1,0:T(2,128)(2,1)S(1)}, u32[]{:S(2)}, u32[]{:S(2)}) async-start(bf16[8,2,8192]{2,1,0:T(2,128)(2,1)} %reshape.371), calls=%async_computation.5 | async-start | bytes 524288 | tf_op jit(solution)/shard_map/all_to_all | solution.py:90
  250.7 4.6 %scatter_custom_fusion.1 = f32[768,2048]{1,0:T(8,128)} fusion(s32[64]{0:T(128)S(1)} %fusion.78, f32[]{:T(128)} %constant.57.clone.1, bf16[1,64,2048]{2,0,1:T(2,128)(2,1)S(1)} %bitcast.178), kind=kCustom, calls=%fused_computation.17 | custom fusion | flops 262144 | bytes 6815748 | tf_op jit(solution)/shard_map/scatter-add | solution.py:84
  255.3 4.9 %convert_element_type.75 = bf16[768,2048]{1,0:T(8,128)(2,1)} convert(f32[768,2048]{1,0:T(8,128)} %scatter_custom_fusion.1) | non-fusion elementwise | flops 1572864 | bytes 9437184 | tf_op jit(solution)/shard_map/convert_element_type | solution.py:85
  261.8 3.2 %collective-permute-start.4 = (bf16[1,64,768]{2,1,0:T(8,128)(2,1)S(1)}, bf16[1,64,768]{2,1,0:T(8,128)(2,1)S(1)}, u32[]{:S(2)}, u32[]{:S(2)}) collective-permute-start(bf16[1,64,768]{2,1,0:T(8,128)(2,1)S(1)} %collective-permute-done.2), channel_id=1, source_target_pairs={{0,28},{4,0},{8,4},{12,8},{16,12},{20,16},{24,20},{28,24},{1,29},{... | collective-permute-start | bytes 294920 | tf_op jit(solution)/shard_map/ppermute | solution.py:17
  267.7 4.4 %collective-permute-done.6 = bf16[1,64,768]{2,1,0:T(8,128)(2,1)S(1)} collective-permute-done((bf16[1,64,768]{2,1,0:T(8,128)(2,1)S(1)}, bf16[1,64,768]{2,1,0:T(8,128)(2,1)S(1)}, u32[]{:S(2)}, u32[]{:S(2)}) %collective-permute-start.6) | collective-permute-done | bytes 98336 | tf_op jit(solution)/shard_map/ppermute | solution.py:15
  (99 shorter events, 61.2 us)
Async XLA Ops:
  7.2 10.4 %copy-start.7 = (s32[1,4,1,16]{3,2,1,0:T(1,128)S(1)}, s32[1,4,1,16]{3,2,1,0:T(1,128)}, u32[]{:S(2)}) copy-start(s32[1,4,1,16]{3,2,1,0:T(1,128)} %param.10) | copy-start | bytes 772
  7.2 48.8 %all-gather.6.cloned.1.call-start = ((), (), s32[]{:S(2)}) async-start(), calls=%async_computation.6 | async-start | bytes 3538944 | tf_op jit(solution)/shard_map/all_gather | solution.py:45
  7.9 86.7 %all-gather.8.cloned.1.call-start = ((), (), s32[]{:S(2)}) async-start(), calls=%async_computation.7 | async-start | bytes 3538944 | tf_op jit(solution)/shard_map/all_gather | solution.py:46
  8.7 124.7 %all-gather.10.cloned.1.call-start = ((), (), s32[]{:S(2)}) async-start(), calls=%async_computation.8 | async-start | bytes 3538944 | tf_op jit(solution)/shard_map/all_gather | solution.py:47
  10.9 30.9 %copy-start.8 = (f32[1,4,1,16]{3,2,1,0:T(1,128)S(1)}, f32[1,4,1,16]{3,2,1,0:T(1,128)}, u32[]{:S(2)}) copy-start(f32[1,4,1,16]{3,2,1,0:T(1,128)} %param.12) | copy-start | bytes 772
  11.8 10.6 %all-to-all-start = ((bf16[4,16,2048]{2,1,0:T(8,128)(2,1)}), bf16[4,16,2048]{2,1,0:T(8,128)(2,1)S(1)}, u32[]{:S(2)}, u32[]{:S(2)}) async-start(bf16[4,16,2048]{2,1,0:T(8,128)(2,1)} %broadcast_multiply_fusion), calls=%async_computation | async-start | bytes 524288 | tf_op jit(solution)/shard_map/all_to_all | solution.py:24
  36.3 18.4 %all-to-all-start.4 = ((bf16[8,2,8192]{2,1,0:T(2,128)(2,1)}), bf16[8,2,8192]{2,1,0:T(2,128)(2,1)S(1)}, u32[]{:S(2)}, u32[]{:S(2)}) async-start(bf16[8,2,8192]{2,1,0:T(2,128)(2,1)} %reshape.369), calls=%async_computation.4 | async-start | bytes 524288 | tf_op jit(solution)/shard_map/all_to_all | solution.py:89
  58.6 74.8 %copy-start.6 = (f32[64,768]{1,0:T(8,128)}, f32[64,768]{1,0:T(8,128)S(1)}, u32[]{:S(2)}) copy-start(f32[64,768]{1,0:T(8,128)S(1)} %fusion.10) | copy-start | bytes 589828
  139.8 9.4 %all-to-all-start.1 = ((bf16[4,2,16384]{2,1,0:T(2,128)(2,1)}), bf16[4,2,16384]{2,1,0:T(2,128)(2,1)S(1)}, u32[]{:S(2)}, u32[]{:S(2)}) async-start(bf16[4,2,16384]{2,1,0:T(2,128)(2,1)} %reshape.365), calls=%async_computation.1 | async-start | bytes 524288 | tf_op jit(solution)/shard_map/all_to_all | solution.py:28
  150.1 5.3 %copy-start.5 = (bf16[768,2048]{1,0:T(8,128)(2,1)S(1)}, bf16[768,2048]{1,0:T(8,128)(2,1)}, u32[]{:S(2)}) copy-start(bf16[768,2048]{1,0:T(8,128)(2,1)} %param.9) | copy-start | bytes 9437188
  162.3 27.1 %copy-start.3 = (bf16[2048,1,768]{2,0,1:T(8,128)(2,1)S(1)}, bf16[2048,1,768]{2,0,1:T(8,128)(2,1)}, u32[]{:S(2)}) copy-start(bf16[2048,1,768]{2,0,1:T(8,128)(2,1)} %all-gather.10.cloned.1.call-done) | copy-start | bytes 9437188
  168.9 20.5 %all-to-all-start.2 = ((bf16[4,16,2048]{2,1,0:T(8,128)(2,1)}), bf16[4,16,2048]{2,1,0:T(8,128)(2,1)}, u32[]{:S(2)}, u32[]{:S(2)}) async-start(bf16[4,16,2048]{2,1,0:T(8,128)(2,1)} %multiply_convert_fusion), calls=%async_computation.2 | async-start | bytes 524288 | tf_op jit(solution)/shard_map/all_to_all | solution.py:24
  191.2 22.9 %copy-start.2 = (bf16[2048,1,768]{2,0,1:T(8,128)(2,1)S(1)}, bf16[2048,1,768]{2,0,1:T(8,128)(2,1)}, u32[]{:S(2)}) copy-start(bf16[2048,1,768]{2,0,1:T(8,128)(2,1)} %all-gather.6.cloned.1.call-done) | copy-start | bytes 9437188
  191.2 48.9 %collective-permute-start.1 = (bf16[1,64,768]{2,1,0:T(8,128)(2,1)S(1)}, bf16[1,64,768]{2,1,0:T(8,128)(2,1)}, u32[]{:S(2)}, u32[]{:S(2)}) collective-permute-start(bf16[1,64,768]{2,1,0:T(8,128)(2,1)S(1)} %bitcast.185), channel_id=1, source_target_pairs={{0,4},{4,8},{8,12},{12,16},{16,20},{20,24},{24,28},{28,0},{1,5},{5... | collective-permute-start | bytes 294920 | tf_op jit(solution)/shard_map/ppermute | solution.py:15
  191.6 48.9 %collective-permute-start = (bf16[1,64,768]{2,1,0:T(8,128)(2,1)S(1)}, bf16[1,64,768]{2,1,0:T(8,128)(2,1)}, u32[]{:S(2)}, u32[]{:S(2)}) collective-permute-start(bf16[1,64,768]{2,1,0:T(8,128)(2,1)S(1)} %bitcast.186), channel_id=1, source_target_pairs={{0,28},{4,0},{8,4},{12,8},{16,12},{20,16},{24,20},{28,24},{1,29},{... | collective-permute-start | bytes 294920 | tf_op jit(solution)/shard_map/ppermute | solution.py:17
  215.2 8.0 %copy-start.4 = (bf16[512,768]{1,0:T(8,128)(2,1)S(1)}, bf16[512,768]{1,0:T(8,128)(2,1)}, u32[]{:S(2)}) copy-start(bf16[512,768]{1,0:T(8,128)(2,1)} %all-gather) | copy-start | bytes 2359300
  218.6 27.5 %all-to-all-start.3 = ((bf16[4,2,16384]{2,1,0:T(2,128)(2,1)}), bf16[4,2,16384]{2,1,0:T(2,128)(2,1)}, u32[]{:S(2)}, u32[]{:S(2)}) async-start(bf16[4,2,16384]{2,1,0:T(2,128)(2,1)} %reshape.367), calls=%async_computation.3 | async-start | bytes 524288 | tf_op jit(solution)/shard_map/all_to_all | solution.py:28
  240.1 20.1 %collective-permute-start.3 = (bf16[1,64,768]{2,1,0:T(8,128)(2,1)}, bf16[1,64,768]{2,1,0:T(8,128)(2,1)}, u32[]{:S(2)}, u32[]{:S(2)}) collective-permute-start(bf16[1,64,768]{2,1,0:T(8,128)(2,1)} %collective-permute-done.1), channel_id=1, source_target_pairs={{0,4},{4,8},{8,12},{12,16},{16,20},{20,24},{24,28},{28,0},{1,5},{5... | collective-permute-start | bytes 294920 | tf_op jit(solution)/shard_map/ppermute | solution.py:15
  240.5 21.3 %collective-permute-start.2 = (bf16[1,64,768]{2,1,0:T(8,128)(2,1)}, bf16[1,64,768]{2,1,0:T(8,128)(2,1)S(1)}, u32[]{:S(2)}, u32[]{:S(2)}) collective-permute-start(bf16[1,64,768]{2,1,0:T(8,128)(2,1)} %collective-permute-done), channel_id=1, source_target_pairs={{0,28},{4,0},{8,4},{12,8},{16,12},{20,16},{24,20},{28,24},{1,29},{... | collective-permute-start | bytes 294920 | tf_op jit(solution)/shard_map/ppermute | solution.py:17
  246.1 28.0 %all-to-all-start.5 = ((bf16[8,2,8192]{2,1,0:T(2,128)(2,1)}), bf16[8,2,8192]{2,1,0:T(2,128)(2,1)S(1)}, u32[]{:S(2)}, u32[]{:S(2)}) async-start(bf16[8,2,8192]{2,1,0:T(2,128)(2,1)} %reshape.371), calls=%async_computation.5 | async-start | bytes 524288 | tf_op jit(solution)/shard_map/all_to_all | solution.py:90
  260.2 6.1 %collective-permute-start.5 = (bf16[1,64,768]{2,1,0:T(8,128)(2,1)}, bf16[1,64,768]{2,1,0:T(8,128)(2,1)S(1)}, u32[]{:S(2)}, u32[]{:S(2)}) collective-permute-start(bf16[1,64,768]{2,1,0:T(8,128)(2,1)} %collective-permute-done.3), channel_id=1, source_target_pairs={{0,4},{4,8},{8,12},{12,16},{16,20},{20,24},{24,28},{28,0},{1,5},{5... | collective-permute-start | bytes 294920 | tf_op jit(solution)/shard_map/ppermute | solution.py:15
  261.8 5.6 %collective-permute-start.4 = (bf16[1,64,768]{2,1,0:T(8,128)(2,1)S(1)}, bf16[1,64,768]{2,1,0:T(8,128)(2,1)S(1)}, u32[]{:S(2)}, u32[]{:S(2)}) collective-permute-start(bf16[1,64,768]{2,1,0:T(8,128)(2,1)S(1)} %collective-permute-done.2), channel_id=1, source_target_pairs={{0,28},{4,0},{8,4},{12,8},{16,12},{20,16},{24,20},{28,24},{1,29},{... | collective-permute-start | bytes 294920 | tf_op jit(solution)/shard_map/ppermute | solution.py:17
  266.2 5.8 %collective-permute-start.6 = (bf16[1,64,768]{2,1,0:T(8,128)(2,1)S(1)}, bf16[1,64,768]{2,1,0:T(8,128)(2,1)S(1)}, u32[]{:S(2)}, u32[]{:S(2)}) collective-permute-start(bf16[1,64,768]{2,1,0:T(8,128)(2,1)S(1)} %collective-permute-done.5), channel_id=1, source_target_pairs={{0,4},{4,8},{8,12},{12,16},{16,20},{20,24},{24,28},{28,0},{1,5},{5... | collective-permute-start | bytes 294920 | tf_op jit(solution)/shard_map/ppermute | solution.py:15
  276.0 8.0 %copy-start.1 = (bf16[768,2048]{1,0:T(8,128)(2,1)S(1)}, bf16[768,2048]{1,0:T(8,128)(2,1)}, u32[]{:S(2)}) copy-start(bf16[768,2048]{1,0:T(8,128)(2,1)} %param.8) | copy-start | bytes 9437188
  (2 other events, 6.8 us)
Sparse Core Ops, SparseCore 0:
  9.7 44.6 all-gather.5
  56.0 38.5 all-gather.7
  96.2 37.1 all-gather.9
